TPU v7x, 32 devices: a whole 2x2x4 slice. The times are simulated.
32 devices in a mesh: groups: 2 (over y), row: 8 (over z, x), col: 2 (over core).
Axes of the slice: x: 2, y: 2, z: 4, core: 2. Of those that a mesh axis runs over, the one named last changes fastest.
Arguments:
- object_slices: float32 [4, 2, 2048, 512], P(None, None, ('groups', 'row'), 'col'), parts along dimension 2, may hold values from -4 to 4
- probe: float32 [16, 2, 128, 128], P('groups'), parts along dimension 0, may hold values from -3 to 3
- taps: float32 [2, 63], replicated, may hold values from -0.5 to 0.5
- measured: float32 [64, 128, 128], P(('groups', 'row', 'col')), parts along dimension 0, may hold values from 0.5 to 16
- positions: int32 [64, 2], P(('groups', 'row', 'col')), parts along dimension 0, may hold values from -64 to 959, as said below
Outputs:
- object_grad: float32 [4, 2, 2048, 512], P(None, None, ('groups', 'row'), 'col'), parts along dimension 2
- new_probe: float32 [16, 2, 16384], P('groups', None, ('row', 'col')), parts along dimension 0
There are 2 independent parts, one for each index of `groups`. A program takes and returns all parts, laid end to end along the dimension named above; an argument that names none is the same for every part. Nothing has to cross between parts.
Inputs may be any that keep to these rules, and one draw needn't show every extreme that they name: `positions`: record r belongs to device d = r // 2 in row-major order over the (row, col) device grid, with tile indices (i, q); its row lies in [i * 128 - 128/2, (i + 1) * 128 - 128/2) and its column in [q * 256 - 128/2, (q + 1) * 256 - 128/2).
All inputs are finite; a program needn't handle non-finite values.
Results may differ from a plain program's by a relative error of at most 0.0003.
Values sent between devices are 32-bit elements; how exact they have to be, the bound alone decides.
No kernel may reach another device: no remote copies, remote signals or barrier semaphores. Data moves between devices by JAX's collectives and lax.ppermute only.
A program may use at most 64 MiB of HBM per device.

v0:
```python
import math
import jax
import jax.numpy as jnp
from jax import lax
from jax.sharding import PartitionSpec as P

highest_mode = lax.Precision.HIGHEST


def from_behind(value, axis, steps):
    count = lax.axis_size(axis)
    first, last = (max(0, -steps), min(count, count - steps))
    return lax.ppermute(value, axis, [(source, source + steps) for source in range(first, last)])


def with_halo(array, sides, width):
    for axis, dim in sides:
        devices, length = (lax.axis_size(axis), array.shape[dim])
        up = [(i, (i + 1) % devices) for i in range(devices - 1)]
        down = [(j, i) for i, j in up]
        last = lax.slice_in_dim(array, length - width, length, axis=dim)
        first = lax.slice_in_dim(array, 0, width, axis=dim)
        before = lax.ppermute(last, axis, up)
        after = lax.ppermute(first, axis, down)
        array = jnp.concatenate([before, array, after], axis=dim)
    return array


def einsum_exact(form, first, second):
    return jnp.einsum(form, first, second, precision=highest_mode)


def make_tables(taps, width):
    reach = taps.shape[1] // 2
    pixel_idx = lax.iota(jnp.int32, width)
    offset = pixel_idx[None, :] - pixel_idx[:, None] + reach
    tap_idx = lax.iota(jnp.int32, taps.shape[1])
    one_hot = (offset[:, :, None] == tap_idx[None, None, :]).astype(jnp.float32)
    band_re = einsum_exact("abt,t->ab", one_hot, taps[0])
    band_im = einsum_exact("abt,t->ab", one_hot, taps[1])
    phase_idx = pixel_idx[:, None] * pixel_idx[None, :] % width
    angle = 2.0 * math.pi / width * phase_idx.astype(jnp.float32)
    norm_factor = 1.0 / math.sqrt(width)
    return (band_re, band_im, jnp.cos(angle) * norm_factor, -jnp.sin(angle) * norm_factor)


def both_sides(mat_re, mat_im, wave_re, wave_im):
    left_re = einsum_exact("ab,kbc->kac", mat_re, wave_re) - einsum_exact(
        "ab,kbc->kac", mat_im, wave_im
    )
    left_im = einsum_exact("ab,kbc->kac", mat_re, wave_im) + einsum_exact(
        "ab,kbc->kac", mat_im, wave_re
    )
    out_re = einsum_exact("kac,dc->kad", left_re, mat_re) - einsum_exact(
        "kac,dc->kad", left_im, mat_im
    )
    out_im = einsum_exact("kac,dc->kad", left_re, mat_im) + einsum_exact(
        "kac,dc->kad", left_im, mat_re
    )
    return (out_re, out_im)


def record_loss(probe, patch, measured_one, tables):
    band_re, band_im, dft_re, dft_im = tables
    wave_re = probe[:, 0]
    wave_im = probe[:, 1]
    layers = patch.shape[0]
    for layer_idx in range(layers):
        obj_re = patch[layer_idx, 0]
        obj_im = patch[layer_idx, 1]
        wave_re, wave_im = (
            wave_re * obj_re - wave_im * obj_im,
            wave_re * obj_im + wave_im * obj_re,
        )
        if layer_idx + 1 < layers:
            wave_re, wave_im = both_sides(band_re, band_im, wave_re, wave_im)
    far_re, far_im = both_sides(dft_re, dft_im, wave_re, wave_im)
    intensity = jnp.sum(far_re * far_re + far_im * far_im, axis=0)
    weight = 1.0 / (8.0 * probe.shape[0])
    return 0.5 * weight * jnp.sum((intensity - measured_one) ** 2)


def accumulate(grid, probe, measured, places, tables, patch_width):
    sizes = (grid.shape[0], 2, patch_width, patch_width)

    def one_record(carry, item):
        grad_grid, grad_probe = carry
        place, measured_one = item
        zero_idx = jnp.zeros((), jnp.int32)
        starts = (zero_idx, zero_idx, place[0], place[1])
        patch = lax.dynamic_slice(grid, starts, sizes)
        grad_wave, grad_patch = jax.grad(record_loss, argnums=(0, 1))(
            probe, patch, measured_one, tables
        )
        current = lax.dynamic_slice(grad_grid, starts, sizes)
        grad_grid = lax.dynamic_update_slice(grad_grid, current + grad_patch, starts)
        return ((grad_grid, grad_probe + grad_wave), None)

    init = (jnp.zeros(grid.shape, jnp.float32), jnp.zeros(probe.shape, jnp.float32))
    (grad_grid, grad_probe), unused = lax.scan(one_record, init, (places, measured))
    return (grad_grid, grad_probe)


def gram_of(first, second):
    stacked = jnp.concatenate([first, second], axis=0)
    col_re = stacked[:, 0]
    col_im = stacked[:, 1]
    gram_re = einsum_exact("ax,bx->ab", col_re, col_re) + einsum_exact("ax,bx->ab", col_im, col_im)
    gram_im = einsum_exact("ax,bx->ab", col_re, col_im) - einsum_exact("ax,bx->ab", col_im, col_re)
    return (gram_re, gram_im)


def complex_cholesky(herm_re, herm_im):
    count = herm_re.shape[0]
    order_idx = lax.iota(jnp.int32, count)
    cols_re = []
    cols_im = []
    for col_idx in range(count):
        numer_re = herm_re[:, col_idx]
        numer_im = herm_im[:, col_idx]
        for prev_idx in range(col_idx):
            vec_re = cols_re[prev_idx]
            vec_im = cols_im[prev_idx]
            pivot_re = vec_re[col_idx]
            pivot_im = vec_im[col_idx]
            numer_re = numer_re - (vec_re * pivot_re + vec_im * pivot_im)
            numer_im = numer_im - (vec_im * pivot_re - vec_re * pivot_im)
        diag_val = jnp.sqrt(numer_re[col_idx])
        below = order_idx > col_idx
        at_diag = order_idx == col_idx
        cols_re.append(
            jnp.where(below, numer_re / diag_val, 0.0) + jnp.where(at_diag, diag_val, 0.0)
        )
        cols_im.append(jnp.where(below, numer_im / diag_val, 0.0))
    return (jnp.stack(cols_re, axis=1), jnp.stack(cols_im, axis=1))


def lower_inverse(low_re, low_im):
    count = low_re.shape[0]
    unit = jnp.eye(count, dtype=low_re.dtype)
    rows_re = []
    rows_im = []
    for row_idx in range(count):
        acc_re = unit[row_idx]
        acc_im = jnp.zeros_like(unit[row_idx])
        for prev_idx in range(row_idx):
            coef_re = low_re[row_idx, prev_idx]
            coef_im = low_im[row_idx, prev_idx]
            acc_re = acc_re - (coef_re * rows_re[prev_idx] - coef_im * rows_im[prev_idx])
            acc_im = acc_im - (coef_re * rows_im[prev_idx] + coef_im * rows_re[prev_idx])
        rows_re.append(acc_re / low_re[row_idx, row_idx])
        rows_im.append(acc_im / low_re[row_idx, row_idx])
    return (jnp.stack(rows_re, axis=0), jnp.stack(rows_im, axis=0))


def orthonormalize(probe_cols, grad_cols, gram_re, gram_im, scale_out):
    modes = probe_cols.shape[0]
    trace_pp = jnp.trace(gram_re[:modes, :modes])
    trace_gg = jnp.trace(gram_re[modes:, modes:])
    factor = 0.5 * jnp.sqrt(trace_pp / (trace_gg + 1e-06))
    new_re = (
        gram_re[:modes, :modes]
        - factor * (gram_re[:modes, modes:] + gram_re[modes:, :modes])
        + factor * factor * gram_re[modes:, modes:]
    )
    new_im = (
        gram_im[:modes, :modes]
        - factor * (gram_im[:modes, modes:] + gram_im[modes:, :modes])
        + factor * factor * gram_im[modes:, modes:]
    )
    low_re, low_im = complex_cholesky(new_re, new_im)
    inv_re, inv_im = lower_inverse(low_re, low_im)
    right_re = inv_re.T
    right_im = -inv_im.T
    moved = probe_cols - factor * grad_cols
    moved_re = moved[:, 0]
    moved_im = moved[:, 1]
    out_re = einsum_exact("kx,kj->jx", moved_re, right_re) - einsum_exact(
        "kx,kj->jx", moved_im, right_im
    )
    out_im = einsum_exact("kx,kj->jx", moved_re, right_im) + einsum_exact(
        "kx,kj->jx", moved_im, right_re
    )
    return jnp.stack([out_re, out_im], axis=1) * scale_out


def fold_axis(grad, dim, half):
    full = grad.shape[dim]
    inner = full - 2 * half
    core = lax.slice_in_dim(grad, half, half + inner, axis=dim)
    for step_by in (1, -1):
        if step_by == 1:
            sent = lax.slice_in_dim(grad, half + inner, full, axis=dim)
        else:
            sent = lax.slice_in_dim(grad, 0, half, axis=dim)
        if dim == 2:
            arrived = from_behind(sent, "row", step_by)
        else:
            arrived = from_behind(sent, "col", step_by)
        widths = [(0, 0)] * grad.ndim
        if step_by == 1:
            widths[dim] = (0, inner - half)
        else:
            widths[dim] = (inner - half, 0)
        core = core + jnp.pad(arrived, widths)
    return core


def per_device(object_slices, probe, taps, measured, positions):
    width = probe.shape[-1]
    half = width // 2
    tile_rows = object_slices.shape[2]
    tile_cols = object_slices.shape[3]
    tables = make_tables(taps, width)
    extended = with_halo(object_slices, (("row", 2), ("col", 3)), half)
    anchor = jnp.stack(
        [lax.axis_index("row") * tile_rows - half, lax.axis_index("col") * tile_cols - half]
    )
    places = positions - anchor[None, :]
    grad_ext, grad_probe = accumulate(extended, probe, measured, places, tables, width)
    folded = fold_axis(fold_axis(grad_ext, 2, half), 3, half)
    modes = probe.shape[0]
    pixels = width * width
    probe_cols = probe.reshape(modes, 2, pixels)
    grad_cols = grad_probe.reshape(modes, 2, pixels)
    share = pixels // (lax.axis_size("row") * lax.axis_size("col"))
    start = lax.axis_index(("row", "col")) * share
    own_probe = lax.dynamic_slice_in_dim(probe_cols, start, share, 2)
    total_grad = lax.psum(grad_cols, ("row", "col"))
    gram_re, gram_im = gram_of(probe_cols, total_grad)
    own_grad = lax.dynamic_slice_in_dim(total_grad, start, share, 2)
    new_probe = orthonormalize(own_probe, own_grad, gram_re, gram_im, float(width))
    return (folded, new_probe)


def solution(mesh):
    placed = (
        P(None, None, ("groups", "row"), "col"),
        P("groups", None, None, None),
        P(),
        P(("groups", "row", "col"), None, None),
        P(("groups", "row", "col"), None),
    )
    return jax.shard_map(
        per_device,
        mesh=mesh,
        in_specs=placed,
        out_specs=(P(None, None, ("groups", "row"), "col"), P("groups", None, ("row", "col"))),
        check_vma=False,
    )
```

profile of v0, /device:TPU:0, one launch (start us, length us, event | category | flops | bytes accessed | tf_op | source)
XLA Modules:
  0.0 651.3 jit_solution(16764180511014686650)
XLA Ops:
  8.5 4.9 collective-permute-start
  18.0 17.8 %collective-permute-done = f32[4,2,64,256]{3,2,1,0:T(8,128)S(1)} collective-permute-done((f32[4,2,64,256]{3,2,1,0:T(8,128)S(1)}, f32[4,2,64,256]{3,2,1,0:T(8,128)S(1)}, u32[]{:S(2)}, u32[]{:S(2)}) %collective-permute-start) | collective-permute-done | bytes 524320 | tf_op jit(solution)/shard_map/ppermute | solution.py:23
  44.0 3.3 fusion.235
  47.3 3.2 fusion.233
  50.5 3.8 pad_maximum_fusion
  56.2 173.7 %while.16 = (s32[]{:T(128)}, f32[4,2,256,384]{3,2,1,0:T(8,128)}, f32[8,2,128,128]{2,3,0,1:T(8,128)}, s32[2,2]{1,0:T(2,128)S(1)}, f32[8,2,128,128]{2,3,0,1:T(8,12...) while((s32[]{:T(128)}, f32[4,2,256,384]{3,2,1,0:T(8,128)}, ...), condition=%wide.region_18.19_spmd.clone.clone, body=%wide.region_0.18_spmd.clone.clone.sunk | while | flops 12914802688 | bytes 137233312 | solution.py:100
  131.2 7.7 %dynamic_update_slice.9 = f32[4,2,256,384]{3,2,1,0:T(8,128)} dynamic-update-slice(f32[4,2,256,384]{3,2,1,0:T(8,128)} %get-tuple-element.615, f32[4,2,128,128]{3,2,1,0:T(8,128)S(1)} %add_add_fusion.2, s32[]{:T(128)} %constant.94.clone.1..sunk, s32[]{:T(128)} %constant.94.clone.1..sunk, s32[]{:T(128)S(6)} %select_n.471, s32[]{:T(128)S(6)} %select_n.472) | dynamic-update-slice | bytes 1048580 | tf_op jit(solution)/shard_map/while/body/eval_jaxpr/dynamic_update_slice | solution.py:96
  210.7 2.4 select_add_fusion.2
  215.2 7.2 %dynamic_update_slice.9 = f32[4,2,256,384]{3,2,1,0:T(8,128)} dynamic-update-slice(f32[4,2,256,384]{3,2,1,0:T(8,128)} %get-tuple-element.615, f32[4,2,128,128]{3,2,1,0:T(8,128)S(1)} %add_add_fusion.2, s32[]{:T(128)} %constant.94.clone.1..sunk, s32[]{:T(128)} %constant.94.clone.1..sunk, s32[]{:T(128)S(6)} %select_n.471, s32[]{:T(128)S(6)} %select_n.472) | dynamic-update-slice | bytes 1048580 | tf_op jit(solution)/shard_map/while/body/eval_jaxpr/dynamic_update_slice | solution.py:96
  233.4 2.7 fusion.298
  236.1 5.0 collective-permute-start.4
  242.4 91.3 %all-reduce.16.cloned.1.call-done = f32[8,2,16384]{2,0,1:T(8,128)} async-done(((f32[8,2,16384]{2,0,1:T(8,128)}), f32[8,2,16384]{2,0,1:T(8,128)}) %all-reduce.16.cloned.1.call-update) | async-done | bytes 1048592 | tf_op jit(solution)/shard_map/psum | solution.py:229
  333.7 2.7 fusion.295
  336.4 2.7 convolution_add_fusion.25
  363.4 3.8 fusion.286
  368.6 3.8 compare_select_fusion.15
  375.1 5.0 fusion.282
  381.5 5.1 compare_select_fusion.13
  389.2 6.2 add_subtract_fusion.2
  396.6 6.2 compare_select_fusion.11
  405.3 7.6 %add_subtract_fusion.1 = f32[8]{0:T(128)S(1)} fusion(f32[8]{0:T(128)S(1)} %compare_select_fusion.11, f32[8]{0:T(128)S(1)} %compare_select_fusion.13, f32[8]{0:T(128)S(1)} %compare_select_fusion.15, f32[8]{0:T(128)S(1)} %compare_select_fusion.17, f32[8]{0:T(128)S(1)} %compare_select_fusion.19, f32[8]{0:T(128)S(1)} %get-tuple-element.459, ...), kind=kLoop, calls=%fused_computation.455 | loop fusion | flops 432 | bytes 516 | tf_op jit(solution)/shard_map/sub | solution.py:126
  414.2 7.6 %compare_select_fusion.9 = f32[8]{0:T(128)S(1)} fusion(f32[8]{0:T(128)S(1)} %compare_select_fusion.11, f32[8]{0:T(128)S(1)} %compare_select_fusion.13, f32[8]{0:T(128)S(1)} %compare_select_fusion.15, f32[8]{0:T(128)S(1)} %compare_select_fusion.17, f32[8]{0:T(128)S(1)} %compare_select_fusion.19, f32[8]{0:T(128)S(1)} %get-tuple-element.460, ...), kind=kLoop, calls=%fused_computation.391 | loop fusion | flops 456 | bytes 520 | tf_op jit(solution)/shard_map/jit(_where)/select_n | solution.py:134
  423.6 8.8 %add_subtract_fusion = f32[8]{0:T(128)S(1)} fusion(f32[8]{0:T(128)S(1)} %compare_select_fusion.9, f32[8]{0:T(128)S(1)} %compare_select_fusion.11, f32[8]{0:T(128)S(1)} %compare_select_fusion.13, f32[8]{0:T(128)S(1)} %compare_select_fusion.15, f32[8]{0:T(128)S(1)} %compare_select_fusion.17, f32[8]{0:T(128)S(1)} %compare_select_fusion.19, ...), kind=kLoop, calls=%fused_computation.454 | loop fusion | flops 512 | bytes 592 | tf_op jit(solution)/shard_map/sub | solution.py:126
  434.1 39.2 %subtract_divide_fusion.1 = (f32[1,8]{0,1:T(8,128)S(1)}, f32[1,8]{0,1:T(8,128)S(1)}, f32[1,8]{0,1:T(8,128)S(1)}, f32[1,8]{0,1:T(8,128)S(1)}, f32[1,8]{0,1:T(8,128)S(1)}) fusion(f32[8,8]{0,1:T(8,128)S(1)} %fusion.251, f32[]{:T(128)} %bitcast.99, f32[]{:T(128)} %bitcast.67, f32[]{:T(128)S(6)} %mul.2504, f32[]{:T(128)} %bitcast.96, f32[]{:T(128)} %bitcast.94, ...), kind=kLoop, calls=%fused_computation.360 | loop fusion | flops 1576 | bytes 720 | tf_op jit(solution)/shard_map/div | solution.py:151
  473.4 27.4 %subtract_divide_fusion.3 = f32[1,8]{0,1:T(8,128)S(1)} fusion(f32[]{:T(128)} %bitcast.81, f32[1,8]{0,1:T(8,128)S(1)} %get-tuple-element.353, f32[1,8]{0,1:T(8,128)S(1)} %get-tuple-element.354, f32[1,8]{0,1:T(8,128)S(1)} %get-tuple-element.355, f32[1,8]{0,1:T(8,128)S(1)} %get-tuple-element.356, f32[]{:T(128)} %bitcast.53, f32[8,8]{0,1:T(8,128)S(1)} %fusion.251, ...), kind=kLoop, calls=%fused_computation.362 | loop fusion | flops 960 | bytes 464 | tf_op jit(solution)/shard_map/div | solution.py:151
  500.8 19.0 %subtract_divide_fusion.5 = f32[1,8]{0,1:T(8,128)S(1)} fusion(f32[1,8]{0,1:T(8,128)S(1)} %get-tuple-element.354, f32[1,8]{0,1:T(8,128)S(1)} %get-tuple-element.355, f32[1,8]{0,1:T(8,128)S(1)} %get-tuple-element.356, f32[1,8]{0,1:T(8,128)S(1)} %get-tuple-element.353, f32[8,8]{0,1:T(8,128)S(1)} %fusion.251, f32[]{:T(128)} %bitcast.65, f32[]{:T(128)} %bitcast.41, ...), kind=kLoop, calls=%fused_computation.365 | loop fusion | flops 608 | bytes 372 | tf_op jit(solution)/shard_map/div | solution.py:151
  519.8 12.3 %subtract_divide_fusion.7 = f32[1,8]{0,1:T(8,128)S(1)} fusion(f32[1,8]{0,1:T(8,128)S(1)} %get-tuple-element.353, f32[1,8]{0,1:T(8,128)S(1)} %get-tuple-element.354, f32[1,8]{0,1:T(8,128)S(1)} %get-tuple-element.355, f32[1,8]{0,1:T(8,128)S(1)} %get-tuple-element.356, f32[8,8]{0,1:T(8,128)S(1)} %fusion.251, f32[]{:T(128)} %bitcast.51, f32[]{:T(128)} %bitcast.31, ...), kind=kLoop, calls=%fused_computation.368 | loop fusion | flops 320 | bytes 288 | tf_op jit(solution)/shard_map/div | solution.py:151
  532.7 27.3 %subtract_divide_fusion.2 = f32[1,8]{0,1:T(8,128)S(1)} fusion(f32[1,8]{0,1:T(8,128)S(1)} %get-tuple-element.353, f32[1,8]{0,1:T(8,128)S(1)} %get-tuple-element.354, f32[1,8]{0,1:T(8,128)S(1)} %get-tuple-element.355, f32[1,8]{0,1:T(8,128)S(1)} %get-tuple-element.356, f32[]{:T(128)} %bitcast.67, f32[]{:T(128)S(6)} %mul.2504, f32[]{:T(128)} %bitcast.81, ...), kind=kLoop, calls=%fused_computation.361 | loop fusion | flops 960 | bytes 432 | tf_op jit(solution)/shard_map/div | solution.py:152
  559.9 19.0 %subtract_divide_fusion.4 = f32[1,8]{0,1:T(8,128)S(1)} fusion(f32[1,8]{0,1:T(8,128)S(1)} %get-tuple-element.353, f32[1,8]{0,1:T(8,128)S(1)} %get-tuple-element.354, f32[1,8]{0,1:T(8,128)S(1)} %get-tuple-element.355, f32[1,8]{0,1:T(8,128)S(1)} %get-tuple-element.356, f32[]{:T(128)} %bitcast.53, f32[]{:T(128)S(6)} %mul.2430, f32[]{:T(128)} %bitcast.65, ...), kind=kLoop, calls=%fused_computation.363 | loop fusion | flops 608 | bytes 340 | tf_op jit(solution)/shard_map/div | solution.py:152
  578.9 7.2 %subtract_divide_fusion.8 = (f32[1,8]{0,1:T(8,128)S(1)}, f32[1,8]{0,1:T(8,128)S(1)}, f32[1,8]{0,1:T(8,128)S(1)}) fusion(f32[1,8]{0,1:T(8,128)S(1)} %get-tuple-element.354, f32[1,8]{0,1:T(8,128)S(1)} %get-tuple-element.355, f32[1,8]{0,1:T(8,128)S(1)} %get-tuple-element.356, f32[]{:T(128)} %bitcast.31, f32[]{:T(128)S(6)} %mul.2318, f32[]{:T(128)} %bitcast.39, ...), kind=kLoop, calls=%fused_computation.369 | loop fusion | flops 192 | bytes 252 | tf_op jit(solution)/shard_map/div | solution.py:152
  586.1 36.6 %subtract_divide_fusion = f32[1,8]{0,1:T(8,128)S(1)} fusion(f32[1,8]{0,1:T(8,128)S(1)} %get-tuple-element.353, f32[1,8]{0,1:T(8,128)S(1)} %get-tuple-element.354, f32[1,8]{0,1:T(8,128)S(1)} %get-tuple-element.355, f32[1,8]{0,1:T(8,128)S(1)} %get-tuple-element.356, f32[]{:T(128)} %bitcast.83, f32[]{:T(128)S(6)} %mul.2550, f32[]{:T(128)} %bitcast.99, ...), kind=kLoop, calls=%fused_computation.359 | loop fusion | flops 1376 | bytes 532 | tf_op jit(solution)/shard_map/div | solution.py:152
  622.8 12.2 %subtract_divide_fusion.6 = f32[1,8]{0,1:T(8,128)S(1)} fusion(f32[1,8]{0,1:T(8,128)S(1)} %get-tuple-element.353, f32[1,8]{0,1:T(8,128)S(1)} %get-tuple-element.354, f32[1,8]{0,1:T(8,128)S(1)} %get-tuple-element.355, f32[1,8]{0,1:T(8,128)S(1)} %get-tuple-element.356, f32[]{:T(128)} %bitcast.41, f32[]{:T(128)S(6)} %mul.2368, f32[]{:T(128)} %bitcast.51, ...), kind=kLoop, calls=%fused_computation.366 | loop fusion | flops 320 | bytes 256 | tf_op jit(solution)/shard_map/div | solution.py:152
  (339 shorter events, 193.8 us)
Async XLA Ops:
  7.2 326.5 %all-reduce.16.cloned.1.call-start = ((), (), s32[]{:S(2)}) async-start(), calls=%async_computation | async-start | bytes 2097152 | tf_op jit(solution)/shard_map/psum | solution.py:229
  8.5 27.2 %collective-permute-start = (f32[4,2,64,256]{3,2,1,0:T(8,128)S(1)}, f32[4,2,64,256]{3,2,1,0:T(8,128)S(1)}, u32[]{:S(2)}, u32[]{:S(2)}) collective-permute-start(f32[4,2,64,256]{3,2,1,0:T(8,128)S(1)} %get-tuple-element.392), channel_id=1, source_target_pairs={{0,2},{2,4},{4,6},{6,8},{8,10},{10,12},{12,14},{1,3},{3,5},{5,7},{... | collective-permute-start | bytes 1572872 | tf_op jit(solution)/shard_map/ppermute | solution.py:23
  13.4 22.7 %collective-permute-start.1 = (f32[4,2,64,256]{3,2,1,0:T(8,128)S(1)}, f32[4,2,64,256]{3,2,1,0:T(8,128)}, u32[]{:S(2)}, u32[]{:S(2)}) collective-permute-start(f32[4,2,64,256]{3,2,1,0:T(8,128)S(1)} %get-tuple-element.393), channel_id=1, source_target_pairs={{2,0},{4,2},{6,4},{8,6},{10,8},{12,10},{14,12},{3,1},{5,3},{7,5},{... | collective-permute-start | bytes 1572872 | tf_op jit(solution)/shard_map/ppermute | solution.py:24
  36.1 6.2 copy-start.23
  37.5 4.9 copy-start.9
  37.5 6.4 copy-start.24
  39.0 11.5 %collective-permute-start.2 = (f32[4,2,256,64]{2,3,1,0:T(8,128)}, f32[4,2,256,64]{2,3,1,0:T(8,128)}, u32[]{:S(2)}, u32[]{:S(2)}) collective-permute-start(f32[4,2,256,64]{2,3,1,0:T(8,128)} %get-tuple-element.388), channel_id=1, source_target_pairs={{0,1},{2,3},{4,5},{6,7},{8,9},{10,11},{12,13},{14,15},{16,17},{18,... | collective-permute-start | bytes 1572872 | tf_op jit(solution)/shard_map/ppermute | solution.py:23
  41.1 9.5 %collective-permute-start.3 = (f32[4,2,256,64]{2,3,1,0:T(8,128)}, f32[4,2,256,64]{2,3,1,0:T(8,128)}, u32[]{:S(2)}, u32[]{:S(2)}) collective-permute-start(f32[4,2,256,64]{2,3,1,0:T(8,128)} %get-tuple-element.389), channel_id=1, source_target_pairs={{1,0},{3,2},{5,4},{7,6},{9,8},{11,10},{13,12},{15,14},{17,16},{19,... | collective-permute-start | bytes 1572872 | tf_op jit(solution)/shard_map/ppermute | solution.py:24
  44.0 6.6 %copy-start.10 = (f32[4,2,64,256]{2,3,1,0:T(8,128)S(1)}, f32[4,2,64,256]{2,3,1,0:T(8,128)}, u32[]{:S(2)}) copy-start(f32[4,2,64,256]{2,3,1,0:T(8,128)} %copy-done.9) | copy-start | bytes 1572868
  56.7 9.2 %copy-start = (f32[8,2,128,128]{2,3,0,1:T(8,128)}, f32[8,2,128,128]{2,3,0,1:T(8,128)S(1)}, u32[]{:S(2)}) copy-start(f32[8,2,128,128]{2,3,0,1:T(8,128)S(1)} %get-tuple-element.634) | copy-start | bytes 3145732 | tf_op jit(solution)/shard_map/while
  63.6 3.4 copy-start.6
  90.6 4.4 copy-start.2
  90.6 4.4 copy-start.3
  97.4 4.5 copy-start.22
  123.2 3.6 copy-start.5
  123.2 3.6 copy-start.7
  139.2 9.2 %copy-start = (f32[8,2,128,128]{2,3,0,1:T(8,128)}, f32[8,2,128,128]{2,3,0,1:T(8,128)S(1)}, u32[]{:S(2)}) copy-start(f32[8,2,128,128]{2,3,0,1:T(8,128)S(1)} %get-tuple-element.634) | copy-start | bytes 3145732 | tf_op jit(solution)/shard_map/while
  146.0 3.4 copy-start.6
  173.3 4.4 copy-start.2
  173.3 4.4 copy-start.3
  180.0 4.5 copy-start.22
  205.9 3.6 copy-start.5
  205.9 3.6 copy-start.7
  209.5 3.7 copy-start.11
  209.5 3.7 copy-start.12
  209.6 3.7 copy-start.13
  209.6 3.7 copy-start.14
  236.1 399.5 %collective-permute-start.4 = (f32[4,2,64,384]{3,2,1,0:T(8,128)}, f32[4,2,64,384]{3,2,1,0:T(8,128)S(1)}, u32[]{:S(2)}, u32[]{:S(2)}) collective-permute-start(f32[4,2,64,384]{3,2,1,0:T(8,128)} %get-tuple-element.386), channel_id=1, source_target_pairs={{0,2},{2,4},{4,6},{6,8},{8,10},{10,12},{12,14},{1,3},{3,5},{5,7},{... | collective-permute-start | bytes 2359304 | tf_op jit(solution)/shard_map/ppermute | solution.py:13
  241.1 394.5 %collective-permute-start.5 = (f32[4,2,64,384]{3,2,1,0:T(8,128)}, f32[4,2,64,384]{3,2,1,0:T(8,128)}, u32[]{:S(2)}, u32[]{:S(2)}) collective-permute-start(f32[4,2,64,384]{3,2,1,0:T(8,128)} %get-tuple-element.387), channel_id=1, source_target_pairs={{2,0},{4,2},{6,4},{8,6},{10,8},{12,10},{14,12},{3,1},{5,3},{7,5},{... | collective-permute-start | bytes 2359304 | tf_op jit(solution)/shard_map/ppermute | solution.py:13
  333.7 8.8 %copy-start.8 = (f32[8,2,16384]{2,0,1:T(8,128)S(1)}, f32[8,2,16384]{2,0,1:T(8,128)}, u32[]{:S(2)}) copy-start(f32[8,2,16384]{2,0,1:T(8,128)} %all-reduce.16.cloned.1.call-done) | copy-start | bytes 3145732
  637.7 3.8 collective-permute-start.6
  639.0 3.8 collective-permute-start.7
  (21 other events, 47.2 us)
Sparse Core Ops, SparseCore 0:
  232.9 100.7 all-reduce.15
where the time goes:
time: 663 us; the launch traced here: 651 us
  other arithmetic  279 us (42%)
  matrix products  135 us (20%)
  waiting for transfers between devices  110 us (17%)
  local copies, waits for them, and re-layouts  59.8 us (9%)
  between operations  30.9 us (5%)
  starting transfers between devices  18.4 us (3%)
  loops' own time  17.8 us (3%)
    dot_general x138, matrix products, einsum_exact(): return jnp.einsum(form, first, second, precision=highest_mode)  135 us
    div x5, other arithmetic, lower_inverse(): rows_im.append(acc_im / low_re[row_idx, row_idx])  102 us
    div x4, other arithmetic, lower_inverse(): rows_re.append(acc_re / low_re[row_idx, row_idx])  97.9 us
    psum x1, waiting for transfers between devices, per_device(): total_grad = lax.psum(grad_cols, ('row', 'col'))  91.3 us
    sub x7, other arithmetic, complex_cholesky(): numer_re = numer_re - (vec_re * pivot_re + vec_im * pivot_im)  34.9 us
    select_n x7, other arithmetic, complex_cholesky(): cols_im.append(jnp.where(below, numer_im / diag_val, 0.0))  26.1 us
    another operation x1, loops' own time, accumulate(): lax.scan(one_record, init, (places, measured))  17.8 us
    ppermute x2, waiting for transfers between devices, with_halo(): before = lax.ppermute(last, axis, up)  17.8 us
  transfers between devices with their start and end apart: 9, of which 3 were waited for; matrix products, arithmetic and copies ran while one was open for 46% of the time, Pallas kernels for 0%

commit v1 on v0

--- a/solution.py
+++ b/solution.py
@@ -226,7 +226,7 @@
     share = pixels // (lax.axis_size("row") * lax.axis_size("col"))
     start = lax.axis_index(("row", "col")) * share
     own_probe = lax.dynamic_slice_in_dim(probe_cols, start, share, 2)
-    total_grad = lax.psum(grad_cols, ("row", "col"))
+    total_grad = lax.psum(lax.psum(grad_cols, "col"), "row")
     gram_re, gram_im = gram_of(probe_cols, total_grad)
     own_grad = lax.dynamic_slice_in_dim(total_grad, start, share, 2)
     new_probe = orthonormalize(own_probe, own_grad, gram_re, gram_im, float(width))

time: 663 us -> 668 us (level)
    psum x1 -> x2, waiting for transfers between devices: 91.3 us -> 70.9 us  [per_device(): total_grad = lax.psum(lax.psum(grad_cols, 'col'), 'row')]
    ppermute x4, waiting for transfers between devices: 1.35 us -> 21.8 us  [from_behind(): lax.ppermute(value, axis, [(source, source + steps) for source in range(f...]
  transfers between devices with their start and end apart: 9 -> 10, of which waited for: 3 -> 5; matrix products, arithmetic and copies ran while one was open for 46% -> 3% of each run, Pallas kernels for 0% -> 0%
where the time goes in v1:
time: 668 us; the launch traced here: 656 us
  other arithmetic  281 us (42%)
  matrix products  135 us (20%)
  waiting for transfers between devices  110 us (16%)
  local copies, waits for them, and re-layouts  60.9 us (9%)
  between operations  30.9 us (5%)
  starting transfers between devices  20.9 us (3%)
  loops' own time  17.1 us (3%)
    dot_general x138, matrix products, einsum_exact(): return jnp.einsum(form, first, second, precision=highest_mode)  135 us
    div x5, other arithmetic, lower_inverse(): rows_im.append(acc_im / low_re[row_idx, row_idx])  103 us
    div x4, other arithmetic, lower_inverse(): rows_re.append(acc_re / low_re[row_idx, row_idx])  97.9 us
    psum x2, waiting for transfers between devices, per_device(): total_grad = lax.psum(lax.psum(grad_cols, 'col'), 'row')  70.9 us
    sub x7, other arithmetic, complex_cholesky(): numer_re = numer_re - (vec_re * pivot_re + vec_im * pivot_im)  35.2 us
    select_n x7, other arithmetic, complex_cholesky(): cols_im.append(jnp.where(below, numer_im / diag_val, 0.0))  26.2 us
    ppermute x4, waiting for transfers between devices, from_behind(): lax.ppermute(value, axis, [(source, source + steps) for source in range(f...  21.8 us
    ppermute x2, waiting for transfers between devices, with_halo(): before = lax.ppermute(last, axis, up)  17.8 us
  transfers between devices with their start and end apart: 10, of which 5 were waited for; matrix products, arithmetic and copies ran while one was open for 3% of the time, Pallas kernels for 0%

profile of v1, /device:TPU:0, one launch (start us, length us, event | category | flops | bytes accessed | tf_op | source)
XLA Modules:
  0.0 656.3 jit_solution(12243490238859473198)
XLA Ops:
  8.5 4.9 collective-permute-start
  18.0 17.8 %collective-permute-done = f32[4,2,64,256]{3,2,1,0:T(8,128)S(1)} collective-permute-done((f32[4,2,64,256]{3,2,1,0:T(8,128)S(1)}, f32[4,2,64,256]{3,2,1,0:T(8,128)S(1)}, u32[]{:S(2)}, u32[]{:S(2)}) %collective-permute-start) | collective-permute-done | bytes 524320 | tf_op jit(solution)/shard_map/ppermute | solution.py:23
  44.0 3.3 fusion.235
  47.3 3.2 fusion.233
  50.6 3.7 pad_maximum_fusion
  56.2 172.9 %while.16 = (s32[]{:T(128)}, f32[4,2,256,384]{3,2,1,0:T(8,128)}, f32[8,2,128,128]{2,3,0,1:T(8,128)}, s32[2,2]{1,0:T(2,128)S(1)}, f32[8,2,128,128]{2,3,0,1:T(8,12...) while((s32[]{:T(128)}, f32[4,2,256,384]{3,2,1,0:T(8,128)}, ...), condition=%wide.region_18.19_spmd.clone.clone, body=%wide.region_0.18_spmd.clone.clone.sunk | while | flops 12914802688 | bytes 137233312 | solution.py:100
  130.8 7.7 %dynamic_update_slice.9 = f32[4,2,256,384]{3,2,1,0:T(8,128)} dynamic-update-slice(f32[4,2,256,384]{3,2,1,0:T(8,128)} %get-tuple-element.615, f32[4,2,128,128]{3,2,1,0:T(8,128)S(1)} %add_add_fusion.2, s32[]{:T(128)} %constant.94.clone.1..sunk, s32[]{:T(128)} %constant.94.clone.1..sunk, s32[]{:T(128)S(6)} %select_n.471, s32[]{:T(128)S(6)} %select_n.472) | dynamic-update-slice | bytes 1048580 | tf_op jit(solution)/shard_map/while/body/eval_jaxpr/dynamic_update_slice | solution.py:96
  214.4 7.2 %dynamic_update_slice.9 = f32[4,2,256,384]{3,2,1,0:T(8,128)} dynamic-update-slice(f32[4,2,256,384]{3,2,1,0:T(8,128)} %get-tuple-element.615, f32[4,2,128,128]{3,2,1,0:T(8,128)S(1)} %add_add_fusion.2, s32[]{:T(128)} %constant.94.clone.1..sunk, s32[]{:T(128)} %constant.94.clone.1..sunk, s32[]{:T(128)S(6)} %select_n.471, s32[]{:T(128)S(6)} %select_n.472) | dynamic-update-slice | bytes 1048580 | tf_op jit(solution)/shard_map/while/body/eval_jaxpr/dynamic_update_slice | solution.py:96
  235.6 5.9 collective-permute-start.4
  242.7 15.8 %all-reduce.17.cloned.1.call-done = f32[8,2,16384]{2,0,1:T(8,128)} async-done(((f32[8,2,16384]{2,0,1:T(8,128)}), f32[8,2,16384]{2,0,1:T(8,128)}) %all-reduce.17.cloned.1.call-update) | async-done | bytes 1048592 | tf_op jit(solution)/shard_map/psum | solution.py:229
  258.6 19.9 %collective-permute-done.4 = f32[4,2,64,384]{3,2,1,0:T(8,128)} collective-permute-done((f32[4,2,64,384]{3,2,1,0:T(8,128)}, f32[4,2,64,384]{3,2,1,0:T(8,128)}, u32[]{:S(2)}, u32[]{:S(2)}) %collective-permute-start.4) | collective-permute-done | bytes 786464 | tf_op jit(solution)/shard_map/ppermute | solution.py:13
  280.3 2.8 collective-permute-start.6
  286.9 2.9 fusion.242
  289.8 55.0 %all-reduce.19.cloned.1.call-done = f32[8,2,16384]{2,0,1:T(8,128)} async-done(((f32[8,2,16384]{2,0,1:T(8,128)}), f32[8,2,16384]{2,0,1:T(8,128)}) %all-reduce.19.cloned.1.call-update) | async-done | bytes 1048592 | tf_op jit(solution)/shard_map/psum | solution.py:229
  375.3 3.7 fusion.286
  380.2 3.7 compare_select_fusion.15
  386.4 4.9 fusion.282
  392.8 4.9 compare_select_fusion.13
  400.3 6.1 add_subtract_fusion.2
  407.5 6.1 compare_select_fusion.11
  416.2 7.7 %add_subtract_fusion.1 = f32[8]{0:T(128)S(1)} fusion(f32[8]{0:T(128)S(1)} %compare_select_fusion.11, f32[8]{0:T(128)S(1)} %compare_select_fusion.13, f32[8]{0:T(128)S(1)} %compare_select_fusion.15, f32[8]{0:T(128)S(1)} %compare_select_fusion.17, f32[8]{0:T(128)S(1)} %compare_select_fusion.19, f32[8]{0:T(128)S(1)} %get-tuple-element.459, ...), kind=kLoop, calls=%fused_computation.455 | loop fusion | flops 432 | bytes 516 | tf_op jit(solution)/shard_map/sub | solution.py:126
  425.3 7.7 %compare_select_fusion.9 = f32[8]{0:T(128)S(1)} fusion(f32[8]{0:T(128)S(1)} %compare_select_fusion.11, f32[8]{0:T(128)S(1)} %compare_select_fusion.13, f32[8]{0:T(128)S(1)} %compare_select_fusion.15, f32[8]{0:T(128)S(1)} %compare_select_fusion.17, f32[8]{0:T(128)S(1)} %compare_select_fusion.19, f32[8]{0:T(128)S(1)} %get-tuple-element.460, ...), kind=kLoop, calls=%fused_computation.391 | loop fusion | flops 456 | bytes 520 | tf_op jit(solution)/shard_map/jit(_where)/select_n | solution.py:134
  434.9 9.0 %add_subtract_fusion = f32[8]{0:T(128)S(1)} fusion(f32[8]{0:T(128)S(1)} %compare_select_fusion.9, f32[8]{0:T(128)S(1)} %compare_select_fusion.11, f32[8]{0:T(128)S(1)} %compare_select_fusion.13, f32[8]{0:T(128)S(1)} %compare_select_fusion.15, f32[8]{0:T(128)S(1)} %compare_select_fusion.17, f32[8]{0:T(128)S(1)} %compare_select_fusion.19, ...), kind=kLoop, calls=%fused_computation.454 | loop fusion | flops 512 | bytes 592 | tf_op jit(solution)/shard_map/sub | solution.py:126
  445.8 39.3 %subtract_divide_fusion.1 = (f32[1,8]{0,1:T(8,128)S(1)}, f32[1,8]{0,1:T(8,128)S(1)}, f32[1,8]{0,1:T(8,128)S(1)}, f32[1,8]{0,1:T(8,128)S(1)}, f32[1,8]{0,1:T(8,128)S(1)}) fusion(f32[8,8]{0,1:T(8,128)S(1)} %fusion.251, f32[]{:T(128)} %bitcast.99, f32[]{:T(128)} %bitcast.67, f32[]{:T(128)S(6)} %mul.2504, f32[]{:T(128)} %bitcast.96, f32[]{:T(128)} %bitcast.94, ...), kind=kLoop, calls=%fused_computation.360 | loop fusion | flops 1576 | bytes 720 | tf_op jit(solution)/shard_map/div | solution.py:151
  485.1 27.2 %subtract_divide_fusion.3 = f32[1,8]{0,1:T(8,128)S(1)} fusion(f32[]{:T(128)} %bitcast.81, f32[1,8]{0,1:T(8,128)S(1)} %get-tuple-element.353, f32[1,8]{0,1:T(8,128)S(1)} %get-tuple-element.354, f32[1,8]{0,1:T(8,128)S(1)} %get-tuple-element.355, f32[1,8]{0,1:T(8,128)S(1)} %get-tuple-element.356, f32[]{:T(128)} %bitcast.53, f32[8,8]{0,1:T(8,128)S(1)} %fusion.251, ...), kind=kLoop, calls=%fused_computation.362 | loop fusion | flops 960 | bytes 464 | tf_op jit(solution)/shard_map/div | solution.py:151
  512.3 19.1 %subtract_divide_fusion.5 = f32[1,8]{0,1:T(8,128)S(1)} fusion(f32[1,8]{0,1:T(8,128)S(1)} %get-tuple-element.354, f32[1,8]{0,1:T(8,128)S(1)} %get-tuple-element.355, f32[1,8]{0,1:T(8,128)S(1)} %get-tuple-element.356, f32[1,8]{0,1:T(8,128)S(1)} %get-tuple-element.353, f32[8,8]{0,1:T(8,128)S(1)} %fusion.251, f32[]{:T(128)} %bitcast.65, f32[]{:T(128)} %bitcast.41, ...), kind=kLoop, calls=%fused_computation.365 | loop fusion | flops 608 | bytes 372 | tf_op jit(solution)/shard_map/div | solution.py:151
  531.3 12.4 %subtract_divide_fusion.7 = f32[1,8]{0,1:T(8,128)S(1)} fusion(f32[1,8]{0,1:T(8,128)S(1)} %get-tuple-element.353, f32[1,8]{0,1:T(8,128)S(1)} %get-tuple-element.354, f32[1,8]{0,1:T(8,128)S(1)} %get-tuple-element.355, f32[1,8]{0,1:T(8,128)S(1)} %get-tuple-element.356, f32[8,8]{0,1:T(8,128)S(1)} %fusion.251, f32[]{:T(128)} %bitcast.51, f32[]{:T(128)} %bitcast.31, ...), kind=kLoop, calls=%fused_computation.368 | loop fusion | flops 320 | bytes 288 | tf_op jit(solution)/shard_map/div | solution.py:151
  544.4 27.3 %subtract_divide_fusion.2 = f32[1,8]{0,1:T(8,128)S(1)} fusion(f32[1,8]{0,1:T(8,128)S(1)} %get-tuple-element.353, f32[1,8]{0,1:T(8,128)S(1)} %get-tuple-element.354, f32[1,8]{0,1:T(8,128)S(1)} %get-tuple-element.355, f32[1,8]{0,1:T(8,128)S(1)} %get-tuple-element.356, f32[]{:T(128)} %bitcast.67, f32[]{:T(128)S(6)} %mul.2504, f32[]{:T(128)} %bitcast.81, ...), kind=kLoop, calls=%fused_computation.361 | loop fusion | flops 960 | bytes 432 | tf_op jit(solution)/shard_map/div | solution.py:152
  571.7 19.0 %subtract_divide_fusion.4 = f32[1,8]{0,1:T(8,128)S(1)} fusion(f32[1,8]{0,1:T(8,128)S(1)} %get-tuple-element.353, f32[1,8]{0,1:T(8,128)S(1)} %get-tuple-element.354, f32[1,8]{0,1:T(8,128)S(1)} %get-tuple-element.355, f32[1,8]{0,1:T(8,128)S(1)} %get-tuple-element.356, f32[]{:T(128)} %bitcast.53, f32[]{:T(128)S(6)} %mul.2430, f32[]{:T(128)} %bitcast.65, ...), kind=kLoop, calls=%fused_computation.363 | loop fusion | flops 608 | bytes 340 | tf_op jit(solution)/shard_map/div | solution.py:152
  590.7 12.4 %subtract_divide_fusion.6 = f32[1,8]{0,1:T(8,128)S(1)} fusion(f32[1,8]{0,1:T(8,128)S(1)} %get-tuple-element.353, f32[1,8]{0,1:T(8,128)S(1)} %get-tuple-element.354, f32[1,8]{0,1:T(8,128)S(1)} %get-tuple-element.355, f32[1,8]{0,1:T(8,128)S(1)} %get-tuple-element.356, f32[]{:T(128)} %bitcast.41, f32[]{:T(128)S(6)} %mul.2368, f32[]{:T(128)} %bitcast.51, ...), kind=kLoop, calls=%fused_computation.366 | loop fusion | flops 320 | bytes 256 | tf_op jit(solution)/shard_map/div | solution.py:152
  603.1 7.5 %subtract_divide_fusion.8 = (f32[1,8]{0,1:T(8,128)S(1)}, f32[1,8]{0,1:T(8,128)S(1)}, f32[1,8]{0,1:T(8,128)S(1)}) fusion(f32[1,8]{0,1:T(8,128)S(1)} %get-tuple-element.354, f32[1,8]{0,1:T(8,128)S(1)} %get-tuple-element.355, f32[1,8]{0,1:T(8,128)S(1)} %get-tuple-element.356, f32[]{:T(128)} %bitcast.31, f32[]{:T(128)S(6)} %mul.2318, f32[]{:T(128)} %bitcast.39, ...), kind=kLoop, calls=%fused_computation.369 | loop fusion | flops 192 | bytes 252 | tf_op jit(solution)/shard_map/div | solution.py:152
  610.6 36.9 %subtract_divide_fusion = f32[1,8]{0,1:T(8,128)S(1)} fusion(f32[1,8]{0,1:T(8,128)S(1)} %get-tuple-element.353, f32[1,8]{0,1:T(8,128)S(1)} %get-tuple-element.354, f32[1,8]{0,1:T(8,128)S(1)} %get-tuple-element.355, f32[1,8]{0,1:T(8,128)S(1)} %get-tuple-element.356, f32[]{:T(128)} %bitcast.83, f32[]{:T(128)S(6)} %mul.2550, f32[]{:T(128)} %bitcast.99, ...), kind=kLoop, calls=%fused_computation.359 | loop fusion | flops 1376 | bytes 532 | tf_op jit(solution)/shard_map/div | solution.py:152
  (346 shorter events, 203.5 us)
Async XLA Ops:
  7.2 251.4 %all-reduce.17.cloned.1.call-start = ((), (), s32[]{:S(2)}) async-start(), calls=%async_computation | async-start | bytes 2097152 | tf_op jit(solution)/shard_map/psum | solution.py:229
  8.5 27.2 %collective-permute-start = (f32[4,2,64,256]{3,2,1,0:T(8,128)S(1)}, f32[4,2,64,256]{3,2,1,0:T(8,128)S(1)}, u32[]{:S(2)}, u32[]{:S(2)}) collective-permute-start(f32[4,2,64,256]{3,2,1,0:T(8,128)S(1)} %get-tuple-element.392), channel_id=1, source_target_pairs={{0,2},{2,4},{4,6},{6,8},{8,10},{10,12},{12,14},{1,3},{3,5},{5,7},{... | collective-permute-start | bytes 1572872 | tf_op jit(solution)/shard_map/ppermute | solution.py:23
  13.4 22.7 %collective-permute-start.1 = (f32[4,2,64,256]{3,2,1,0:T(8,128)S(1)}, f32[4,2,64,256]{3,2,1,0:T(8,128)}, u32[]{:S(2)}, u32[]{:S(2)}) collective-permute-start(f32[4,2,64,256]{3,2,1,0:T(8,128)S(1)} %get-tuple-element.393), channel_id=1, source_target_pairs={{2,0},{4,2},{6,4},{8,6},{10,8},{12,10},{14,12},{3,1},{5,3},{7,5},{... | collective-permute-start | bytes 1572872 | tf_op jit(solution)/shard_map/ppermute | solution.py:24
  36.1 6.3 copy-start.25
  37.5 4.9 copy-start.10
  37.5 6.5 copy-start.26
  39.0 11.5 %collective-permute-start.2 = (f32[4,2,256,64]{2,3,1,0:T(8,128)}, f32[4,2,256,64]{2,3,1,0:T(8,128)}, u32[]{:S(2)}, u32[]{:S(2)}) collective-permute-start(f32[4,2,256,64]{2,3,1,0:T(8,128)} %get-tuple-element.388), channel_id=1, source_target_pairs={{0,1},{2,3},{4,5},{6,7},{8,9},{10,11},{12,13},{14,15},{16,17},{18,... | collective-permute-start | bytes 1572872 | tf_op jit(solution)/shard_map/ppermute | solution.py:23
  41.1 9.5 %collective-permute-start.3 = (f32[4,2,256,64]{2,3,1,0:T(8,128)}, f32[4,2,256,64]{2,3,1,0:T(8,128)}, u32[]{:S(2)}, u32[]{:S(2)}) collective-permute-start(f32[4,2,256,64]{2,3,1,0:T(8,128)} %get-tuple-element.389), channel_id=1, source_target_pairs={{1,0},{3,2},{5,4},{7,6},{9,8},{11,10},{13,12},{15,14},{17,16},{19,... | collective-permute-start | bytes 1572872 | tf_op jit(solution)/shard_map/ppermute | solution.py:24
  44.0 6.6 %copy-start.11 = (f32[4,2,64,256]{2,3,1,0:T(8,128)S(1)}, f32[4,2,64,256]{2,3,1,0:T(8,128)}, u32[]{:S(2)}) copy-start(f32[4,2,64,256]{2,3,1,0:T(8,128)} %copy-done.10) | copy-start | bytes 1572868
  56.7 8.8 %copy-start = (f32[8,2,128,128]{2,3,0,1:T(8,128)}, f32[8,2,128,128]{2,3,0,1:T(8,128)S(1)}, u32[]{:S(2)}) copy-start(f32[8,2,128,128]{2,3,0,1:T(8,128)S(1)} %get-tuple-element.634) | copy-start | bytes 3145732 | tf_op jit(solution)/shard_map/while
  90.2 4.4 copy-start.2
  90.2 4.4 copy-start.3
  97.0 4.5 copy-start.24
  122.8 3.6 copy-start.5
  122.8 3.6 copy-start.7
  138.7 8.8 %copy-start = (f32[8,2,128,128]{2,3,0,1:T(8,128)}, f32[8,2,128,128]{2,3,0,1:T(8,128)S(1)}, u32[]{:S(2)}) copy-start(f32[8,2,128,128]{2,3,0,1:T(8,128)S(1)} %get-tuple-element.634) | copy-start | bytes 3145732 | tf_op jit(solution)/shard_map/while
  172.5 4.4 copy-start.2
  172.5 4.4 copy-start.3
  179.2 4.5 copy-start.24
  205.1 3.6 copy-start.5
  208.7 3.7 copy-start.13
  208.7 3.7 copy-start.14
  208.7 3.7 copy-start.15
  208.7 3.7 copy-start.16
  229.2 5.2 copy-start.9
  234.3 110.6 %all-reduce.19.cloned.1.call-start = ((), (), s32[]{:S(2)}) async-start(), calls=%async_computation.1 | async-start | bytes 2097152 | tf_op jit(solution)/shard_map/psum | solution.py:229
  235.6 42.9 %collective-permute-start.4 = (f32[4,2,64,384]{3,2,1,0:T(8,128)}, f32[4,2,64,384]{3,2,1,0:T(8,128)}, u32[]{:S(2)}, u32[]{:S(2)}) collective-permute-start(f32[4,2,64,384]{3,2,1,0:T(8,128)} %get-tuple-element.386), channel_id=1, source_target_pairs={{0,2},{2,4},{4,6},{6,8},{8,10},{10,12},{12,14},{1,3},{3,5},{5,7},{... | collective-permute-start | bytes 2359304 | tf_op jit(solution)/shard_map/ppermute | solution.py:13
  241.5 37.1 %collective-permute-start.5 = (f32[4,2,64,384]{3,2,1,0:T(8,128)}, f32[4,2,64,384]{3,2,1,0:T(8,128)}, u32[]{:S(2)}, u32[]{:S(2)}) collective-permute-start(f32[4,2,64,384]{3,2,1,0:T(8,128)} %get-tuple-element.387), channel_id=1, source_target_pairs={{2,0},{4,2},{6,4},{8,6},{10,8},{12,10},{14,12},{3,1},{5,3},{7,5},{... | collective-permute-start | bytes 2359304 | tf_op jit(solution)/shard_map/ppermute | solution.py:13
  258.6 25.8 %copy-start.23 = (f32[8,2,128,128]{3,2,1,0:T(8,128)S(1)}, f32[8,2,128,128]{3,2,1,0:T(8,128)}, u32[]{:S(2)}) copy-start(f32[8,2,128,128]{3,2,1,0:T(8,128)} %param.8) | copy-start | bytes 3145732
  280.3 4.8 collective-permute-start.6
  283.1 3.8 collective-permute-start.7
  344.9 8.8 %copy-start.8 = (f32[8,2,16384]{2,0,1:T(8,128)S(1)}, f32[8,2,16384]{2,0,1:T(8,128)}, u32[]{:S(2)}) copy-start(f32[8,2,16384]{2,0,1:T(8,128)} %all-reduce.19.cloned.1.call-done) | copy-start | bytes 3145732
  (24 other events, 57.8 us)
Sparse Core Ops, SparseCore 0:
  234.4 24.1 all-reduce.16
  262.5 82.3 all-reduce.18
